TPU v7x, 32 devices: a whole 2x2x4 slice. The times are simulated.
32 devices in a mesh: freq: 8 (over z, x), pair: 4 (over y, core).
Axes of the slice: x: 2, y: 2, z: 4, core: 2. Of those that a mesh axis runs over, the one named last changes fastest.
Arguments:
- samples: bfloat16 [2048, 8, 2, 1024], P(('freq', 'pair')), may hold values from -6 to 6
- rfi_flags: int32 [8, 1024], P('freq'), may hold values 0 or 1
- feed_map: int32 [2048], replicated, may hold values from 0 to 2047, each once
Outputs:
- visibilities: bfloat16 [8, 2, 2048, 2048], P('freq', None, 'pair')
Inputs may be any that keep to these rules, and one draw needn't show every extreme that they name: `feed_map`: each of the 2048 feeds is assigned to exactly one slot.
All inputs are finite; a program needn't handle non-finite values. No bound on the sum of `rfi_flags` on one device may be relied on, other than what follows from the above.
Results may differ from a plain program's by a relative error of at most 0.001.
Values may be sent and summed in bfloat16 or wider, within the bound.
No kernel may reach another device: no remote copies, remote signals or barrier semaphores. Data moves between devices by JAX's collectives and lax.ppermute only.
A program may use at most 64 MiB of HBM per device.

v0:
```python
import jax
import jax.numpy as jnp
from jax import lax
from jax.sharding import PartitionSpec as P


def local(samples, rfi_flags, feed_map):
    n_pair = lax.axis_size("pair")
    n_freq = lax.axis_size("freq")
    member = lax.axis_index("pair")
    keep_mask = (1 - rfi_flags).astype(jnp.bfloat16)
    shard_feeds = samples.shape[0]
    turned = lax.all_to_all(samples, "freq", split_axis=1, concat_axis=0, tiled=True)
    turned = turned * keep_mask[None, :, None, :]
    kept = lax.all_gather(turned, "pair", axis=0, tiled=True)
    shard_index = feed_map // shard_feeds
    within = feed_map % shard_feeds
    position = (
        shard_index % n_pair * (n_freq * shard_feeds) + shard_index // n_pair * shard_feeds + within
    )
    feed_count = kept.shape[0]
    steps_time = kept.shape[3]
    row_count = feed_count // n_pair
    inverse = 1.0 / steps_time
    feeds_all = kept[:, 0].reshape(feed_count, 2 * steps_time)
    columns = jnp.take(feeds_all, position, axis=0)
    own_rows = lax.dynamic_slice_in_dim(columns, member * row_count, row_count, 0)
    rotated_rows = jnp.concatenate([own_rows[:, steps_time:], -own_rows[:, :steps_time]], axis=1)
    stacked = jnp.concatenate([own_rows, rotated_rows], axis=0)
    product = lax.dot_general(
        stacked, columns, (((1,), (1,)), ((), ())), preferred_element_type=jnp.float32
    )
    results = [(product * inverse).astype(jnp.bfloat16).reshape(2, row_count, columns.shape[0])]
    computed = jnp.stack(results, axis=0)
    return computed


def solution(mesh):
    in_specs = (P(("freq", "pair"), None, None, None), P("freq", None), P())
    out_specs = P("freq", None, "pair", None)
    return jax.shard_map(local, mesh=mesh, in_specs=in_specs, out_specs=out_specs, check_vma=False)
```

profile of v0, /device:TPU:0, one launch (start us, length us, event | category | flops | bytes accessed | tf_op | source)
XLA Modules:
  0.0 202.3 jit_solution(14040332480941497455)
XLA Ops:
  6.5 0.0 copy-start.2
  6.5 4.1 %copy.6 = bf16[64,8,2,1024]{3,0,2,1:T(8,128)(2,1)} copy(bf16[64,8,2,1024]{3,2,1,0:T(2,128)(2,1)} %param.3) | data formatting | bytes 4194304 | tf_op args[0]
  10.6 0.0 copy-start.1
  10.6 7.4 %all-to-all-start = ((bf16[64,8,2,1024]{3,0,2,1:T(8,128)(2,1)}), bf16[64,8,2,1024]{3,0,2,1:T(8,128)(2,1)S(1)}, u32[]{:S(2)}, u32[]{:S(2)}) async-start(bf16[64,8,2,1024]{3,0,2,1:T(8,128)(2,1)} %copy.6), calls=%async_computation | async-start | bytes 4194304 | tf_op jit(solution)/shard_map/all_to_all | solution.py:13
  18.0 0.0 all-gather.2.cloned.1.call-start
  18.1 0.0 copy-done.2
  18.1 48.2 %all-to-all-done = bf16[64,8,2,1024]{3,0,2,1:T(8,128)(2,1)S(1)} async-done(((bf16[64,8,2,1024]{3,0,2,1:T(8,128)(2,1)}), bf16[64,8,2,1024]{3,0,2,1:T(8,128)(2,1)S(1)}, u32[]{:S(2)}, u32[]{:S(2)}) %all-to-all-start) | async-done | bytes 2097184 | tf_op jit(solution)/shard_map/all_to_all | solution.py:13
  66.3 0.2 copy.7
  66.4 1.6 bitcast_multiply_fusion
  68.0 0.0 all-gather.2.cloned.1.call-update
  68.1 0.0 copy-done.1
  68.1 57.4 %all-gather.2.cloned.1.call-done = bf16[2048,1,2,1024]{3,0,2,1:T(8,128)(2,1)} async-done(((bf16[512,1,2,1024]{3,0,2,1:T(8,128)(2,1)}), bf16[2048,1,2,1024]{3,0,2,1:T(8,128)(2,1)}) %all-gather.2.cloned.1.call-update) | async-done | bytes 8388624 | tf_op jit(solution)/shard_map/all_gather | solution.py:15
  125.6 16.4 %copy.8 = bf16[2048,1,2,1024]{3,2,0,1:T(2,128)(2,1)} copy(bf16[2048,1,2,1024]{3,0,2,1:T(8,128)(2,1)} %all-gather.2.cloned.1.call-done) | data formatting | bytes 16777216 | tf_op jit(solution)/shard_map/all_gather | solution.py:15
  142.0 10.1 %copy.9 = bf16[256,8,2,1024]{3,1,2,0:T(8,128)(2,1)} copy(bf16[256,8,2,1024]{3,2,1,0:T(2,128)(2,1)} %bitcast.13) | data formatting | bytes 16777216
  152.1 20.8 %gather_fusion = bf16[2048,2048]{1,0:T(8,128)(2,1)} fusion(bf16[2048,2048]{1,0:T(8,128)(2,1)} %bitcast.12, s32[2048]{0:T(1024)S(1)} %broadcast_clamp_fusion), kind=kCustom, calls=%fused_computation | custom fusion | bytes 16785408 | tf_op jit(solution)/shard_map/jit(_take)/gather | solution.py:26
  172.9 7.5 %broadcast_select_fusion = bf16[2048,2048]{1,0:T(8,128)(2,1)} fusion(bf16[2048,2048]{1,0:T(8,128)(2,1)} %gather_fusion, pred[2048]{0:T(1024)(128)(4,1)S(1)} %get-tuple-element.5), kind=kLoop, calls=%fused_computation.2 | loop fusion | flops 4194304 | bytes 16779264 | tf_op jit(solution)/shard_map/jit(_take)/select_n | solution.py:26
  180.4 0.0 copy-start
  180.4 1.9 constant_dynamic-slice_fusion
  182.3 2.2 %fusion.16 = (bf16[512,1024]{1,0:T(8,128)(2,1)S(1)}, bf16[512,1024]{1,0:T(8,128)(2,1)S(1)}) fusion(bf16[2048,2048]{1,0:T(8,128)(2,1)} %broadcast_select_fusion, s32[]{:T(128)S(6)} %select_n.36, s32[]{:T(128)S(6)} %add.37), kind=kLoop, calls=%fused_computation.38 | loop fusion | flops 1572864 | bytes 4194312 | tf_op jit(solution)/shard_map/slice | solution.py:28
  184.4 0.6 copy-done
  185.0 10.4 %multiply_convert_fusion = bf16[1024,2048]{1,0:T(8,128)(2,1)} fusion(bf16[2048,2048]{1,0:T(8,128)(2,1)S(1)} %copy-done, bf16[512,1024]{1,0:T(8,128)(2,1)S(1)} %get-tuple-element.8, bf16[512,1024]{1,0:T(8,128)(2,1)S(1)} %get-tuple-element.7, bf16[512,2048]{1,0:T(8,128)(2,1)S(1)} %constant_dynamic-slice_fusion), kind=kOutput, calls=%fused_computation.1 | convolution fusion | flops 8606711808 | bytes 16777216 | tf_op jit(solution)/shard_map/dot_general | solution.py:30
  (3 shorter events, 0.1 us)
Async XLA Ops:
  6.5 11.5 %copy-start.2 = (s32[1,1024]{1,0:T(1,128)S(1)}, s32[1,1024]{1,0:T(1,128)}, u32[]{:S(2)}) copy-start(s32[1,1024]{1,0:T(1,128)} %param.4) | copy-start | bytes 12292
  10.6 57.5 %copy-start.1 = (s32[2048]{0:T(1024)S(1)}, s32[2048]{0:T(1024)}, u32[]{:S(2)}) copy-start(s32[2048]{0:T(1024)} %param.5) | copy-start | bytes 24580
  10.6 55.7 %all-to-all-start = ((bf16[64,8,2,1024]{3,0,2,1:T(8,128)(2,1)}), bf16[64,8,2,1024]{3,0,2,1:T(8,128)(2,1)S(1)}, u32[]{:S(2)}, u32[]{:S(2)}) async-start(bf16[64,8,2,1024]{3,0,2,1:T(8,128)(2,1)} %copy.6), calls=%async_computation | async-start | bytes 4194304 | tf_op jit(solution)/shard_map/all_to_all | solution.py:13
  18.0 107.5 %all-gather.2.cloned.1.call-start = ((), (), s32[]{:S(2)}) async-start(), calls=%async_computation.1 | async-start | bytes 10485760 | tf_op jit(solution)/shard_map/all_gather | solution.py:15
  180.4 4.6 %copy-start = (bf16[2048,2048]{1,0:T(8,128)(2,1)S(1)}, bf16[2048,2048]{1,0:T(8,128)(2,1)}, u32[]{:S(2)}) copy-start(bf16[2048,2048]{1,0:T(8,128)(2,1)} %broadcast_select_fusion) | copy-start | bytes 25165828
Sparse Core Ops, SparseCore 0:
  68.2 57.3 all-gather.1
where the time goes:
time: 203 us; the launch traced here: 202 us
  waiting for transfers between devices  106 us (52%)
  local copies, waits for them, and re-layouts  54.1 us (27%)
  between operations  13.5 us (7%)
  other arithmetic  11.3 us (6%)
  matrix products  10.4 us (5%)
  starting transfers between devices  7.45 us (4%)
    all_gather x1, waiting for transfers between devices, local(): kept = lax.all_gather(turned, 'pair', axis=0, tiled=True)  57.4 us
    all_to_all x1, waiting for transfers between devices, local(): lax.all_to_all(samples, 'freq', split_axis=1, concat_axis=0, tiled=True)  48.2 us
    gather x1, local copies, waits for them, and re-layouts, local(): columns = jnp.take(feeds_all, position, axis=0)  20.8 us
    all_gather x1, local copies, waits for them, and re-layouts, local(): kept = lax.all_gather(turned, 'pair', axis=0, tiled=True)  16.4 us
    unnamed x8, local copies, waits for them, and re-layouts  14.8 us
    dot_general x1, matrix products, local(): lax.dot_general(stacked, columns, (((1,), (1,)), ((), ())), preferred_ele...  10.4 us
    select_n x1, other arithmetic, local(): columns = jnp.take(feeds_all, position, axis=0)  7.45 us
    all_to_all x1, starting transfers between devices, local(): lax.all_to_all(samples, 'freq', split_axis=1, concat_axis=0, tiled=True)  7.41 us
  transfers between devices with their start and end apart: 2, of which 2 were waited for; matrix products, arithmetic and copies ran while one was open for 0% of the time, Pallas kernels for 0%

commit v1 on v0

--- a/solution.py
+++ b/solution.py
@@ -10,7 +10,19 @@
     member = lax.axis_index("pair")
     keep_mask = (1 - rfi_flags).astype(jnp.bfloat16)
     shard_feeds = samples.shape[0]
-    turned = lax.all_to_all(samples, "freq", split_axis=1, concat_axis=0, tiled=True)
+    ways, here = (lax.axis_size("freq"), lax.axis_index("freq"))
+    width = samples.shape[1] // ways
+    shape = list(samples.shape)
+    shape[1] = width
+    height = shape[0]
+    shape[0] = height * ways
+    full = jnp.zeros(shape, samples.dtype)
+    for mask in range(ways):
+        part = lax.dynamic_slice_in_dim(samples, (here ^ mask) * width, width, axis=1)
+        if mask:
+            part = lax.ppermute(part, "freq", [(d, d ^ mask) for d in range(ways)])
+        full = lax.dynamic_update_slice_in_dim(full, part, (here ^ mask) * height, axis=0)
+    turned = full
     turned = turned * keep_mask[None, :, None, :]
     kept = lax.all_gather(turned, "pair", axis=0, tiled=True)
     shard_index = feed_map // shard_feeds

time: 203 us -> 187 us (0.921)
  waiting for transfers between devices: 106 us -> 90.6 us
  local copies, waits for them, and re-layouts: 54.1 us -> 44.9 us
  starting transfers between devices: 7.45 us -> 13.8 us
    all_to_all x1 -> x0, waiting for transfers between devices: 48.2 us -> none  [local(): lax.all_to_all(samples, 'freq', split_axis=1, concat_axis=0, tiled=True)]
    ppermute x0 -> x7, waiting for transfers between devices: none -> 25.7 us  [local(): part = lax.ppermute(part, 'freq', [(d, d ^ mask) for d in range(ways)])]
    all_gather x1 -> x0, local copies, waits for them, and re-layouts: 16.4 us -> none  [local(): kept = lax.all_gather(turned, 'pair', axis=0, tiled=True)]
    ppermute x0 -> x7, starting transfers between devices: none -> 13.8 us  [local(): part = lax.ppermute(part, 'freq', [(d, d ^ mask) for d in range(ways)])]
    all_gather x1, waiting for transfers between devices: 57.4 us -> 64.9 us  [local(): kept = lax.all_gather(turned, 'pair', axis=0, tiled=True)]
    all_to_all x1 -> x0, starting transfers between devices: 7.41 us -> none  [local(): lax.all_to_all(samples, 'freq', split_axis=1, concat_axis=0, tiled=True)]
    dynamic_update_slice x0 -> x7, local copies, waits for them, and re-layouts: none -> 6.19 us  [local(): lax.dynamic_update_slice_in_dim(full, part, (here ^ mask) * height, axis=0)]
    dynamic_slice x0 -> x1, local copies, waits for them, and re-layouts: none -> 2.92 us  [local(): lax.dynamic_slice_in_dim(samples, (here ^ mask) * width, width, axis=1)]
  transfers between devices with their start and end apart: 2 -> 8, of which waited for: 2 -> 5; matrix products, arithmetic and copies ran while one was open for 0% -> 3% of each run, Pallas kernels for 0% -> 0%
where the time goes in v1:
time: 187 us; the launch traced here: 186 us
  waiting for transfers between devices  90.6 us (48%)
  local copies, waits for them, and re-layouts  44.9 us (24%)
  starting transfers between devices  13.8 us (7%)
  between operations  13.5 us (7%)
  other arithmetic  12.8 us (7%)
  matrix products  10.4 us (6%)
    all_gather x1, waiting for transfers between devices, local(): kept = lax.all_gather(turned, 'pair', axis=0, tiled=True)  64.9 us
    ppermute x7, waiting for transfers between devices, local(): part = lax.ppermute(part, 'freq', [(d, d ^ mask) for d in range(ways)])  25.7 us
    gather x1, local copies, waits for them, and re-layouts, local(): columns = jnp.take(feeds_all, position, axis=0)  21 us
    ppermute x7, starting transfers between devices, local(): part = lax.ppermute(part, 'freq', [(d, d ^ mask) for d in range(ways)])  13.8 us
    unnamed x9, local copies, waits for them, and re-layouts  11.9 us
    dot_general x1, matrix products, local(): lax.dot_general(stacked, columns, (((1,), (1,)), ((), ())), preferred_ele...  10.4 us
    select_n x1, other arithmetic, local(): columns = jnp.take(feeds_all, position, axis=0)  7.45 us
    dynamic_update_slice x7, local copies, waits for them, and re-layouts, local(): lax.dynamic_update_slice_in_dim(full, part, (here ^ mask) * height, axis=0)  6.19 us
  transfers between devices with their start and end apart: 8, of which 5 were waited for; matrix products, arithmetic and copies ran while one was open for 3% of the time, Pallas kernels for 0%

profile of v1, /device:TPU:0, one launch (start us, length us, event | category | flops | bytes accessed | tf_op | source)
XLA Modules:
  0.0 186.1 jit_solution(1252524181165227011)
XLA Ops:
  6.5 1.1 broadcast_in_dim.17
  8.1 2.9 %constant_dynamic-slice_fusion.1 = (bf16[64,1,2,1024]{3,2,1,0:T(2,128)(2,1)S(1)}, bf16[64,1,2,1024]{3,2,1,0:T(2,128)(2,1)S(1)}, bf16[64,1,2,1024]{3,2,1,0:T(2,12...) fusion(bf16[64,8,2,1024]{3,2,1,0:T(2,128)(2,1)S(1)} %copy-done., ...), kind=kLoop, calls=%fused_computation.37 | loop fusion | bytes 4194340 | tf_op jit(solution)/shard_map/dynamic_slice | solution.py:21
  11.1 3.0 %collective-permute-start = (bf16[64,1,2,1024]{3,2,1,0:T(2,128)(2,1)}, bf16[64,1,2,1024]{3,2,1,0:T(2,128)(2,1)}, u32[]{:S(2)}, u32[]{:S(2)}) collective-permute-start(bf16[64,1,2,1024]{3,2,1,0:T(2,128)(2,1)} %get-tuple-element.14), channel_id=1, source_target_pairs={{0,4},{4,0},{8,12},{12,8},{16,20},{20,16},{24,28},{28,24},{1,5},{5... | collective-permute-start | bytes 786440 | tf_op jit(solution)/shard_map/ppermute | solution.py:23
  14.0 1.6 collective-permute-start.1
  15.6 3.0 %collective-permute-start.3 = (bf16[64,1,2,1024]{3,2,1,0:T(2,128)(2,1)S(1)}, bf16[64,1,2,1024]{3,2,1,0:T(2,128)(2,1)}, u32[]{:S(2)}, u32[]{:S(2)}) collective-permute-start(bf16[64,1,2,1024]{3,2,1,0:T(2,128)(2,1)S(1)} %get-tuple-element.11), channel_id=1, source_target_pairs={{0,16},{4,20},{8,24},{12,28},{16,0},{20,4},{24,8},{28,12},{1,17},{... | collective-permute-start | bytes 786440 | tf_op jit(solution)/shard_map/ppermute | solution.py:23
  18.6 1.3 collective-permute-start.4
  20.6 3.8 %collective-permute-start.5 = (bf16[64,1,2,1024]{3,2,1,0:T(2,128)(2,1)S(1)}, bf16[64,1,2,1024]{3,2,1,0:T(2,128)(2,1)S(1)}, u32[]{:S(2)}, u32[]{:S(2)}) collective-permute-start(bf16[64,1,2,1024]{3,2,1,0:T(2,128)(2,1)S(1)} %get-tuple-element.16), channel_id=1, source_target_pairs={{0,24},{4,28},{8,16},{12,20},{16,8},{20,12},{24,0},{28,4},{1,25},{... | collective-permute-start | bytes 786440 | tf_op jit(solution)/shard_map/ppermute | solution.py:23
  24.5 1.2 constant_dynamic-update-slice_fusion.6
  25.6 8.3 %collective-permute-done.1 = bf16[64,1,2,1024]{3,2,1,0:T(2,128)(2,1)} collective-permute-done((bf16[64,1,2,1024]{3,2,1,0:T(2,128)(2,1)}, bf16[64,1,2,1024]{3,2,1,0:T(2,128)(2,1)}, u32[]{:S(2)}, u32[]{:S(2)}) %collective-permute-start.1) | collective-permute-done | bytes 262176 | tf_op jit(solution)/shard_map/ppermute | solution.py:23
  33.9 1.1 collective-permute-start.6
  35.1 1.2 constant_dynamic-update-slice_fusion.5
  36.2 1.1 collective-permute-done.2
  37.3 1.2 constant_dynamic-update-slice_fusion.4
  38.5 1.2 constant_dynamic-update-slice_fusion.3
  39.6 15.6 %collective-permute-done.4 = bf16[64,1,2,1024]{3,2,1,0:T(2,128)(2,1)} collective-permute-done((bf16[64,1,2,1024]{3,2,1,0:T(2,128)(2,1)S(1)}, bf16[64,1,2,1024]{3,2,1,0:T(2,128)(2,1)}, u32[]{:S(2)}, u32[]{:S(2)}) %collective-permute-start.4) | collective-permute-done | bytes 262176 | tf_op jit(solution)/shard_map/ppermute | solution.py:23
  55.2 1.2 constant_dynamic-update-slice_fusion.2
  56.8 3.1 %broadcast_multiply_fusion = bf16[512,1,2,1024]{3,2,1,0:T(2,128)(2,1)} fusion(bf16[512,1,2,1024]{3,2,1,0:T(2,128)(2,1)S(1)} %constant_dynamic-update-slice_fusion, bf16[1024]{0:T(1024)(128)(2,1)S(1)} %convert_reduce_fusion), kind=kLoop, calls=%fused_computation.9 | loop fusion | flops 1048576 | bytes 4196352 | tf_op jit(solution)/shard_map/mul | solution.py:26
  60.7 64.9 %all-gather.2.cloned.1.call-done = bf16[2048,1,2,1024]{3,2,1,0:T(2,128)(2,1)} async-done(((bf16[512,1,2,1024]{3,2,1,0:T(2,128)(2,1)}), bf16[2048,1,2,1024]{3,2,1,0:T(2,128)(2,1)}) %all-gather.2.cloned.1.call-update) | async-done | bytes 8388624 | tf_op jit(solution)/shard_map/all_gather | solution.py:27
  125.6 10.1 %copy.12 = bf16[256,8,2,1024]{3,1,2,0:T(8,128)(2,1)} copy(bf16[256,8,2,1024]{3,2,1,0:T(2,128)(2,1)} %bitcast.6) | data formatting | bytes 16777216
  135.7 21.0 %gather_fusion = bf16[2048,2048]{1,0:T(8,128)(2,1)} fusion(bf16[2048,2048]{1,0:T(8,128)(2,1)} %bitcast.5, s32[2048]{0:T(1024)S(1)} %broadcast_clamp_fusion), kind=kCustom, calls=%fused_computation | custom fusion | bytes 16785408 | tf_op jit(solution)/shard_map/jit(_take)/gather | solution.py:38
  156.7 7.5 %broadcast_select_fusion = bf16[2048,2048]{1,0:T(8,128)(2,1)} fusion(bf16[2048,2048]{1,0:T(8,128)(2,1)} %gather_fusion, pred[2048]{0:T(1024)(128)(4,1)S(1)} %get-tuple-element.5), kind=kLoop, calls=%fused_computation.2 | loop fusion | flops 4194304 | bytes 16779264 | tf_op jit(solution)/shard_map/jit(_take)/select_n | solution.py:38
  164.2 1.9 %constant_dynamic-slice_fusion = bf16[512,2048]{1,0:T(8,128)(2,1)S(1)} fusion(bf16[2048,2048]{1,0:T(8,128)(2,1)} %broadcast_select_fusion, s32[]{:T(128)S(6)} %select_n.100), kind=kLoop, calls=%fused_computation.35 | loop fusion | bytes 4194308 | tf_op jit(solution)/shard_map/dynamic_slice | solution.py:39
  166.0 2.2 %fusion.16 = (bf16[512,1024]{1,0:T(8,128)(2,1)S(1)}, bf16[512,1024]{1,0:T(8,128)(2,1)S(1)}) fusion(bf16[2048,2048]{1,0:T(8,128)(2,1)} %broadcast_select_fusion, s32[]{:T(128)S(6)} %select_n.100, s32[]{:T(128)S(6)} %add.101), kind=kLoop, calls=%fused_computation.53 | loop fusion | flops 1572864 | bytes 4194312 | tf_op jit(solution)/shard_map/slice | solution.py:40
  168.8 10.4 %multiply_convert_fusion = bf16[1024,2048]{1,0:T(8,128)(2,1)} fusion(bf16[2048,2048]{1,0:T(8,128)(2,1)S(1)} %copy-done, bf16[512,1024]{1,0:T(8,128)(2,1)S(1)} %get-tuple-element.8, bf16[512,1024]{1,0:T(8,128)(2,1)S(1)} %get-tuple-element.7, bf16[512,2048]{1,0:T(8,128)(2,1)S(1)} %constant_dynamic-slice_fusion), kind=kOutput, calls=%fused_computation.1 | convolution fusion | flops 8606711808 | bytes 16777216 | tf_op jit(solution)/shard_map/dot_general | solution.py:42
  (20 shorter events, 3.0 us)
Async XLA Ops:
  6.5 119.1 %all-gather.2.cloned.1.call-start = ((), (), s32[]{:S(2)}) async-start(), calls=%async_computation | async-start | bytes 10485760 | tf_op jit(solution)/shard_map/all_gather | solution.py:27
  6.5 1.6 copy-start.1
  8.1 11.7 %copy-start.3 = (s32[1,1024]{1,0:T(1,128)S(1)}, s32[1,1024]{1,0:T(1,128)}, u32[]{:S(2)}) copy-start(s32[1,1024]{1,0:T(1,128)} %param.4) | copy-start | bytes 12292
  11.1 9.6 %collective-permute-start = (bf16[64,1,2,1024]{3,2,1,0:T(2,128)(2,1)}, bf16[64,1,2,1024]{3,2,1,0:T(2,128)(2,1)}, u32[]{:S(2)}, u32[]{:S(2)}) collective-permute-start(bf16[64,1,2,1024]{3,2,1,0:T(2,128)(2,1)} %get-tuple-element.14), channel_id=1, source_target_pairs={{0,4},{4,0},{8,12},{12,8},{16,20},{20,16},{24,28},{28,24},{1,5},{5... | collective-permute-start | bytes 786440 | tf_op jit(solution)/shard_map/ppermute | solution.py:23
  14.0 19.9 %collective-permute-start.1 = (bf16[64,1,2,1024]{3,2,1,0:T(2,128)(2,1)}, bf16[64,1,2,1024]{3,2,1,0:T(2,128)(2,1)}, u32[]{:S(2)}, u32[]{:S(2)}) collective-permute-start(bf16[64,1,2,1024]{3,2,1,0:T(2,128)(2,1)} %get-tuple-element.13), channel_id=1, source_target_pairs={{0,8},{4,12},{8,0},{12,4},{16,24},{20,28},{24,16},{28,20},{1,9},{5... | collective-permute-start | bytes 786440 | tf_op jit(solution)/shard_map/ppermute | solution.py:23
  15.6 21.7 %collective-permute-start.2 = (bf16[64,1,2,1024]{3,2,1,0:T(2,128)(2,1)S(1)}, bf16[64,1,2,1024]{3,2,1,0:T(2,128)(2,1)}, u32[]{:S(2)}, u32[]{:S(2)}) collective-permute-start(bf16[64,1,2,1024]{3,2,1,0:T(2,128)(2,1)S(1)} %get-tuple-element.12), channel_id=1, source_target_pairs={{0,12},{4,8},{8,4},{12,0},{16,28},{20,24},{24,20},{28,16},{1,13},{... | collective-permute-start | bytes 786440 | tf_op jit(solution)/shard_map/ppermute | solution.py:23
  15.6 22.8 %collective-permute-start.3 = (bf16[64,1,2,1024]{3,2,1,0:T(2,128)(2,1)S(1)}, bf16[64,1,2,1024]{3,2,1,0:T(2,128)(2,1)}, u32[]{:S(2)}, u32[]{:S(2)}) collective-permute-start(bf16[64,1,2,1024]{3,2,1,0:T(2,128)(2,1)S(1)} %get-tuple-element.11), channel_id=1, source_target_pairs={{0,16},{4,20},{8,24},{12,28},{16,0},{20,4},{24,8},{28,12},{1,17},{... | collective-permute-start | bytes 786440 | tf_op jit(solution)/shard_map/ppermute | solution.py:23
  18.6 36.6 %collective-permute-start.4 = (bf16[64,1,2,1024]{3,2,1,0:T(2,128)(2,1)S(1)}, bf16[64,1,2,1024]{3,2,1,0:T(2,128)(2,1)}, u32[]{:S(2)}, u32[]{:S(2)}) collective-permute-start(bf16[64,1,2,1024]{3,2,1,0:T(2,128)(2,1)S(1)} %get-tuple-element.10), channel_id=1, source_target_pairs={{0,20},{4,16},{8,28},{12,24},{16,4},{20,0},{24,12},{28,8},{1,21},{... | collective-permute-start | bytes 786440 | tf_op jit(solution)/shard_map/ppermute | solution.py:23
  20.6 35.7 %collective-permute-start.5 = (bf16[64,1,2,1024]{3,2,1,0:T(2,128)(2,1)S(1)}, bf16[64,1,2,1024]{3,2,1,0:T(2,128)(2,1)S(1)}, u32[]{:S(2)}, u32[]{:S(2)}) collective-permute-start(bf16[64,1,2,1024]{3,2,1,0:T(2,128)(2,1)S(1)} %get-tuple-element.16), channel_id=1, source_target_pairs={{0,24},{4,28},{8,16},{12,20},{16,8},{20,12},{24,0},{28,4},{1,25},{... | collective-permute-start | bytes 786440 | tf_op jit(solution)/shard_map/ppermute | solution.py:23
  33.9 22.7 %collective-permute-start.6 = (bf16[64,1,2,1024]{3,2,1,0:T(2,128)(2,1)S(1)}, bf16[64,1,2,1024]{3,2,1,0:T(2,128)(2,1)S(1)}, u32[]{:S(2)}, u32[]{:S(2)}) collective-permute-start(bf16[64,1,2,1024]{3,2,1,0:T(2,128)(2,1)S(1)} %get-tuple-element.9), channel_id=1, source_target_pairs={{0,28},{4,24},{8,20},{12,16},{16,12},{20,8},{24,4},{28,0},{1,29},{... | collective-permute-start | bytes 786440 | tf_op jit(solution)/shard_map/ppermute | solution.py:23
  59.9 0.7 copy-start.2
  164.2 4.6 %copy-start = (bf16[2048,2048]{1,0:T(8,128)(2,1)S(1)}, bf16[2048,2048]{1,0:T(8,128)(2,1)}, u32[]{:S(2)}) copy-start(bf16[2048,2048]{1,0:T(8,128)(2,1)} %broadcast_select_fusion) | copy-start | bytes 25165828
Sparse Core Ops, SparseCore 0:
  60.1 65.4 all-gather.1
